TPU v7x, 512 devices: a whole 4x8x8 slice. The times are simulated.
512 devices in a mesh: gx: 16 (over y_hi, z), gy: 4 (over y_lo), gz: 8 (over x, core).
Axes of the slice: x: 4, y: 8 (y_hi: 2, y_lo: 4; y = y_hi * 4 + y_lo), z: 8, core: 2. Of those that a mesh axis runs over, the one named last changes fastest.
Arguments:
- field: float32 [4, 128, 512, 512], P(None, ('gx', 'gz'), 'gy'), may hold values from -6 to 6
- brick_order: int32 [32], replicated, may hold values from 0 to 31, each once
- start_first: float32 [128, 32], replicated, may hold values from -6 to 6
- start_second: float32 [512, 32], replicated, may hold values from -6 to 6
- start_third: float32 [512, 32], replicated, may hold values from -6 to 6
Outputs:
- core: float32 [128, 32, 32], P(('gx', 'gy'), 'gz')
Inputs may be any that keep to these rules, and one draw needn't show every extreme that they name: `brick_order`: each of 0 to 31 appears exactly once.
All inputs are finite; a program needn't handle non-finite values.
Results may differ from a plain program's by a relative error of at most 0.0003.
Values sent between devices are 32-bit elements; how exact they have to be, the bound alone decides.
No kernel may reach another device: no remote copies, remote signals or barrier semaphores. Data moves between devices by JAX's collectives and lax.ppermute only.
A program may use at most 64 MiB of HBM per device.

v0:
```python
import jax
import jax.numpy as jnp
from jax import lax
from jax.sharding import PartitionSpec as P

ITERS = 2
highest = lax.Precision.HIGHEST


def orthonormal(columns):
    inner_gram = jnp.dot(columns.T, columns, precision=highest)
    factor_low = jnp.linalg.cholesky(inner_gram)
    return jax.scipy.linalg.solve_triangular(factor_low, columns.T, lower=True).T


def subspace(gram_mat, initial):
    current = initial
    for repeat in range(ITERS):
        current = orthonormal(jnp.dot(gram_mat, current, precision=highest))
    return current


def shards(field, brick_order, start_first, start_second, start_third):
    species, rows_x, cells_y, cells_z = field.shape
    count_gx = lax.axis_size("gx")
    count_gy = lax.axis_size("gy")
    count_gz = lax.axis_size("gz")
    brick_count = brick_order.shape[0]
    brick_len = cells_z // count_gz
    small_len = cells_z // brick_count
    cut_y = cells_y // count_gx
    onehot = (brick_order[:, None] == lax.iota(jnp.int32, brick_count)[None, :]).astype(jnp.float32)
    stored = field.reshape(species, rows_x, cells_y, brick_count, small_len)
    placed = jnp.einsum("sxybc,bg->sxygc", stored, onehot, precision=highest).reshape(
        species, rows_x, cells_y, cells_z
    )
    taper = 0.5 + 1.5 * lax.iota(jnp.float32, cells_z) / (cells_z - 1)
    placed = placed * taper
    grid_block = lax.all_to_all(placed, "gz", split_axis=3, concat_axis=1, tiled=True)
    spread = lax.all_to_all(grid_block, "gx", split_axis=2, concat_axis=1, tiled=True)
    local_first = jnp.einsum("sxyz,swyz->xw", spread, spread, precision=highest)
    gram_first = lax.psum(local_first, ("gx", "gy", "gz"))
    factor_first = subspace(gram_first, start_first)
    rank_one = factor_first.shape[1]
    after_first = jnp.einsum("sxyz,xr->sryz", spread, factor_first, precision=highest)
    after_first = after_first.reshape(species * rank_one, cut_y, brick_len)
    regrouped = lax.all_to_all(after_first, ("gx", "gy"), split_axis=0, concat_axis=1, tiled=True)
    merged_rows = regrouped.shape[0]
    regrouped = regrouped.reshape(merged_rows, count_gx, count_gy, cut_y, brick_len)
    second_fibres = jnp.transpose(regrouped, (0, 2, 1, 3, 4)).reshape(
        merged_rows, count_gy * count_gx * cut_y, brick_len
    )
    local_second = jnp.einsum("myz,muz->yu", second_fibres, second_fibres, precision=highest)
    gram_second = lax.psum(local_second, ("gx", "gy", "gz"))
    factor_second = subspace(gram_second, start_second)
    after_second = jnp.einsum("myz,yq->mqz", second_fibres, factor_second, precision=highest)
    third_fibres = lax.all_to_all(after_second, "gz", split_axis=1, concat_axis=2, tiled=True)
    local_third = jnp.einsum("mqz,mqw->zw", third_fibres, third_fibres, precision=highest)
    gram_third = lax.psum(local_third, ("gx", "gy", "gz"))
    factor_third = subspace(gram_third, start_third)
    return jnp.einsum("mqz,zt->mqt", third_fibres, factor_third, precision=highest)


def solution(mesh):
    in_specs = (P(None, ("gx", "gz"), "gy", None), P(), P(), P(), P())
    out_specs = P(("gx", "gy"), "gz", None)
    return jax.shard_map(shards, mesh=mesh, in_specs=in_specs, out_specs=out_specs, check_vma=False)
```

profile of v0, /device:TPU:24, one launch (start us, length us, event | category | flops | bytes accessed | tf_op | source)
XLA Modules:
  0.0 976.2 jit_solution(7257902330931354419)
XLA Ops:
  10.6 20.2 %all_to_all.69 = f32[4,1,128,512]{2,0,1,3:T(4,128)S(1)} all-to-all(f32[4,1,128,512]{2,0,1,3:T(4,128)S(1)} %copy.38), channel_id=1, replica_groups=mesh['gx'=16,'gy'=4,'gz'=8] {'gz'}, dimensions={3} | all-to-all | bytes 2097152 | tf_op jit(solution)/shard_map/all_to_all | solution.py:39
  34.0 39.6 %all_to_all.70 = f32[16,1,16384]{2,1,0:T(1,128)S(1)} all-to-all(f32[16,1,16384]{2,1,0:T(1,128)S(1)} %reshape.62), channel_id=1, replica_groups=mesh['gx'=16,'gy'=4,'gz'=8] {'gx'}, dimensions={0} | all-to-all | bytes 2097152 | tf_op jit(solution)/shard_map/all_to_all | solution.py:40
  74.1 3.1 reduce.4
  78.1 2.6 copy.42
  82.9 2.4 convolution_bitcast_fusion.6
  85.4 256.2 %all-reduce.4.cloned.1.call-done = f32[128,128]{1,0:T(8,128)} async-done(((f32[128,128]{1,0:T(8,128)}), f32[128,128]{1,0:T(8,128)}) %all-reduce.4.cloned.1.call-update) | async-done | bytes 65552 | tf_op jit(solution)/shard_map/psum | solution.py:42
  342.9 2.9 cholesky.104
  347.2 2.4 custom-call.12
  351.2 2.9 cholesky.115
  355.5 2.4 custom-call.13
  358.2 2.9 convolution_bitcast_fusion.3
  361.8 20.5 %all_to_all.71 = f32[64,1,1024]{2,1,0:T(1,128)S(1)} all-to-all(f32[64,1,1024]{2,1,0:T(1,128)S(1)} %reshape.64), channel_id=1, replica_groups=mesh['gx'=16,'gy'=4,'gz'=8] {'gx','gy'}, dimensions={0} | all-to-all | bytes 524288 | tf_op jit(solution)/shard_map/all_to_all | solution.py:47
  385.9 266.8 %all-reduce.6.cloned.1.call-done = f32[512,512]{1,0:T(8,128)} async-done(((f32[512,512]{1,0:T(8,128)}), f32[512,512]{1,0:T(8,128)}) %all-reduce.6.cloned.1.call-update) | async-done | bytes 1048592 | tf_op jit(solution)/shard_map/psum | solution.py:54
  652.7 2.4 fusion.41
  655.3 2.9 cholesky.126
  659.7 2.4 custom-call.14
  663.8 2.9 cholesky.137
  668.2 2.4 custom-call.15
  671.4 9.2 all_to_all.72
  683.6 267.3 %all-reduce.8.cloned.1.call-done = f32[512,512]{1,0:T(8,128)} async-done(((f32[512,512]{1,0:T(8,128)}), f32[512,512]{1,0:T(8,128)}) %all-reduce.8.cloned.1.call-update) | async-done | bytes 1048592 | tf_op jit(solution)/shard_map/psum | solution.py:59
  953.5 2.9 cholesky.148
  957.8 2.4 custom-call.16
  961.9 2.9 cholesky.159
  966.1 2.4 custom-call.17
  (92 shorter events, 37.3 us)
Async XLA Ops:
  6.5 646.1 %copy-start = (f32[512,32]{0,1:T(8,128)S(1)}, f32[512,32]{0,1:T(8,128)}, u32[]{:S(2)}) copy-start(f32[512,32]{0,1:T(8,128)} %param.13) | copy-start | bytes 196612
  6.5 1.6 copy-start.5
  6.5 335.1 %all-reduce.4.cloned.1.call-start = ((), (), s32[]{:S(2)}) async-start(), calls=%async_computation.4 | async-start | bytes 131072 | tf_op jit(solution)/shard_map/psum | solution.py:42
  80.7 260.9 %copy-start.4 = (f32[128,32]{0,1:T(8,128)S(1)}, f32[128,32]{0,1:T(8,128)}, u32[]{:S(2)}) copy-start(f32[128,32]{0,1:T(8,128)} %param.12) | copy-start | bytes 49156
  85.4 567.3 %all-reduce.6.cloned.1.call-start = ((), (), s32[]{:S(2)}) async-start(), calls=%async_computation.5 | async-start | bytes 2097152 | tf_op jit(solution)/shard_map/psum | solution.py:54
  385.8 565.0 %all-reduce.8.cloned.1.call-start = ((), (), s32[]{:S(2)}) async-start(), calls=%async_computation.6 | async-start | bytes 2097152 | tf_op jit(solution)/shard_map/psum | solution.py:59
  652.7 9.8 %copy-start.1 = (f32[512,512]{1,0:T(8,128)S(1)}, f32[512,512]{1,0:T(8,128)}, u32[]{:S(2)}) copy-start(f32[512,512]{1,0:T(8,128)} %all-reduce.6.cloned.1.call-done) | copy-start | bytes 3145732
  662.4 288.4 %copy-start.3 = (f32[512,32]{0,1:T(8,128)S(1)}, f32[512,32]{0,1:T(8,128)}, u32[]{:S(2)}) copy-start(f32[512,32]{0,1:T(8,128)} %param.14) | copy-start | bytes 196612
  950.8 9.6 copy-start.2
Sparse Core Ops, SparseCore 0:
  85.5 256.0 all-reduce.3
  386.0 266.6 all-reduce.5
  683.7 267.0 all-reduce.7
where the time goes:
time: 977 us; the launch traced here: 976 us
  waiting for transfers between devices  790 us (81%)
  blocking collectives  89.5 us (9%)
  other arithmetic  45.7 us (5%)
  matrix products  23.3 us (2%)
  local copies, waits for them, and re-layouts  13.7 us (1%)
  between operations  13.5 us (1%)
    psum x1, waiting for transfers between devices, shards(): gram_third = lax.psum(local_third, ('gx', 'gy', 'gz'))  267 us
    psum x1, waiting for transfers between devices, shards(): gram_second = lax.psum(local_second, ('gx', 'gy', 'gz'))  267 us
    psum x1, waiting for transfers between devices, shards(): gram_first = lax.psum(local_first, ('gx', 'gy', 'gz'))  256 us
    all_to_all x1, blocking collectives, shards(): lax.all_to_all(grid_block, 'gx', split_axis=2, concat_axis=1, tiled=True)  39.6 us
    another operation x18, other arithmetic, orthonormal(): factor_low = jnp.linalg.cholesky(inner_gram)  21.9 us
    all_to_all x1, blocking collectives, shards(): lax.all_to_all(after_first, ('gx', 'gy'), split_axis=0, concat_axis=1, ti...  20.5 us
    all_to_all x1, blocking collectives, shards(): lax.all_to_all(placed, 'gz', split_axis=3, concat_axis=1, tiled=True)  20.2 us
  transfers between devices with their start and end apart: 3, of which 3 were waited for; matrix products, arithmetic and copies ran while one was open for 0% of the time, Pallas kernels for 0%

commit v1 on v0

--- a/solution.py
+++ b/solution.py
@@ -44,7 +44,15 @@
     rank_one = factor_first.shape[1]
     after_first = jnp.einsum("sxyz,xr->sryz", spread, factor_first, precision=highest)
     after_first = after_first.reshape(species * rank_one, cut_y, brick_len)
-    regrouped = lax.all_to_all(after_first, ("gx", "gy"), split_axis=0, concat_axis=1, tiled=True)
+    regrouped = jnp.concatenate(
+        lax.all_to_all(
+            jnp.stack(jnp.split(after_first, lax.axis_size(("gx", "gy")), axis=0)),
+            ("gx", "gy"),
+            0,
+            0,
+        ),
+        axis=1,
+    )
     merged_rows = regrouped.shape[0]
     regrouped = regrouped.reshape(merged_rows, count_gx, count_gy, cut_y, brick_len)
     second_fibres = jnp.transpose(regrouped, (0, 2, 1, 3, 4)).reshape(

time: 977 us -> 978 us (level)
  no operation moved by 1% of the time
where the time goes in v1:
time: 978 us; the launch traced here: 977 us
  waiting for transfers between devices  790 us (81%)
  blocking collectives  89.7 us (9%)
  other arithmetic  45.7 us (5%)
  matrix products  23.3 us (2%)
  between operations  14 us (1%)
  local copies, waits for them, and re-layouts  13.9 us (1%)
    psum x1, waiting for transfers between devices, shards(): gram_third = lax.psum(local_third, ('gx', 'gy', 'gz'))  267 us
    psum x1, waiting for transfers between devices, shards(): gram_second = lax.psum(local_second, ('gx', 'gy', 'gz'))  267 us
    psum x1, waiting for transfers between devices, shards(): gram_first = lax.psum(local_first, ('gx', 'gy', 'gz'))  256 us
    all_to_all x1, blocking collectives, shards(): lax.all_to_all(grid_block, 'gx', split_axis=2, concat_axis=1, tiled=True)  39.6 us
    another operation x18, other arithmetic, orthonormal(): factor_low = jnp.linalg.cholesky(inner_gram)  21.9 us
    all_to_all x1, blocking collectives, shards(): lax.all_to_all(jnp.stack(jnp.split(after_first, lax.axis_size(('gx', 'gy'...  20.7 us
    all_to_all x1, blocking collectives, shards(): lax.all_to_all(placed, 'gz', split_axis=3, concat_axis=1, tiled=True)  20.2 us
  transfers between devices with their start and end apart: 3, of which 3 were waited for; matrix products, arithmetic and copies ran while one was open for 0% of the time, Pallas kernels for 0%

profile of v1, /device:TPU:24, one launch (start us, length us, event | category | flops | bytes accessed | tf_op | source)
XLA Modules:
  0.0 977.2 jit_solution(6537090241458984467)
XLA Ops:
  10.6 20.2 %all_to_all.59 = f32[4,1,128,512]{2,0,1,3:T(4,128)S(1)} all-to-all(f32[4,1,128,512]{2,0,1,3:T(4,128)S(1)} %copy.38), channel_id=1, replica_groups=mesh['gx'=16,'gy'=4,'gz'=8] {'gz'}, dimensions={3} | all-to-all | bytes 2097152 | tf_op jit(solution)/shard_map/all_to_all | solution.py:39
  34.0 39.6 %all_to_all.60 = f32[16,1,16384]{2,1,0:T(1,128)S(1)} all-to-all(f32[16,1,16384]{2,1,0:T(1,128)S(1)} %reshape.61), channel_id=1, replica_groups=mesh['gx'=16,'gy'=4,'gz'=8] {'gx'}, dimensions={0} | all-to-all | bytes 2097152 | tf_op jit(solution)/shard_map/all_to_all | solution.py:40
  74.1 3.1 reduce.4
  78.1 2.6 copy.42
  82.9 2.4 convolution_bitcast_fusion.6
  85.4 256.2 %all-reduce.4.cloned.1.call-done = f32[128,128]{1,0:T(8,128)} async-done(((f32[128,128]{1,0:T(8,128)}), f32[128,128]{1,0:T(8,128)}) %all-reduce.4.cloned.1.call-update) | async-done | bytes 65552 | tf_op jit(solution)/shard_map/psum | solution.py:42
  342.9 2.9 cholesky.104
  347.2 2.4 custom-call.12
  351.2 2.9 cholesky.115
  355.5 2.4 custom-call.13
  358.2 2.9 convolution_bitcast_fusion.3
  362.5 20.7 %all_to_all.61 = f32[64,1,1024]{2,1,0:T(1,128)S(1)} all-to-all(f32[64,1,1024]{2,1,0:T(1,128)S(1)} %reshape.63), channel_id=1, replica_groups=mesh['gx'=16,'gy'=4,'gz'=8] {'gx','gy'}, dimensions={0} | all-to-all | bytes 524288 | tf_op jit(solution)/shard_map/all_to_all | solution.py:48
  386.8 266.8 %all-reduce.6.cloned.1.call-done = f32[512,512]{1,0:T(8,128)} async-done(((f32[512,512]{1,0:T(8,128)}), f32[512,512]{1,0:T(8,128)}) %all-reduce.6.cloned.1.call-update) | async-done | bytes 1048592 | tf_op jit(solution)/shard_map/psum | solution.py:62
  656.3 2.9 cholesky.126
  660.7 2.4 custom-call.14
  664.8 2.9 cholesky.137
  669.2 2.4 custom-call.15
  672.4 9.2 all_to_all.62
  684.6 267.3 %all-reduce.8.cloned.1.call-done = f32[512,512]{1,0:T(8,128)} async-done(((f32[512,512]{1,0:T(8,128)}), f32[512,512]{1,0:T(8,128)}) %all-reduce.8.cloned.1.call-update) | async-done | bytes 1048592 | tf_op jit(solution)/shard_map/psum | solution.py:67
  951.9 2.4 fusion.45
  954.5 2.9 cholesky.148
  958.8 2.4 custom-call.16
  962.9 2.9 cholesky.159
  967.2 2.4 custom-call.17
  (156 shorter events, 37.5 us)
Async XLA Ops:
  6.5 647.1 %copy-start = (f32[512,32]{0,1:T(8,128)S(1)}, f32[512,32]{0,1:T(8,128)}, u32[]{:S(2)}) copy-start(f32[512,32]{0,1:T(8,128)} %param.13) | copy-start | bytes 196612
  6.5 1.6 copy-start.5
  6.5 335.1 %all-reduce.4.cloned.1.call-start = ((), (), s32[]{:S(2)}) async-start(), calls=%async_computation.4 | async-start | bytes 131072 | tf_op jit(solution)/shard_map/psum | solution.py:42
  80.7 260.9 %copy-start.4 = (f32[128,32]{0,1:T(8,128)S(1)}, f32[128,32]{0,1:T(8,128)}, u32[]{:S(2)}) copy-start(f32[128,32]{0,1:T(8,128)} %param.12) | copy-start | bytes 49156
  85.4 568.3 %all-reduce.6.cloned.1.call-start = ((), (), s32[]{:S(2)}) async-start(), calls=%async_computation.5 | async-start | bytes 2097152 | tf_op jit(solution)/shard_map/psum | solution.py:62
  386.8 565.1 %all-reduce.8.cloned.1.call-start = ((), (), s32[]{:S(2)}) async-start(), calls=%async_computation.6 | async-start | bytes 2097152 | tf_op jit(solution)/shard_map/psum | solution.py:67
  653.7 9.8 copy-start.1
  663.4 288.5 %copy-start.3 = (f32[512,32]{0,1:T(8,128)S(1)}, f32[512,32]{0,1:T(8,128)}, u32[]{:S(2)}) copy-start(f32[512,32]{0,1:T(8,128)} %param.14) | copy-start | bytes 196612
  951.9 9.6 copy-start.2
Sparse Core Ops, SparseCore 0:
  85.5 256.0 all-reduce.3
  386.9 266.7 all-reduce.5
  684.7 267.1 all-reduce.7

commit v2 on v0

--- a/solution.py
+++ b/solution.py
@@ -39,7 +39,7 @@
     grid_block = lax.all_to_all(placed, "gz", split_axis=3, concat_axis=1, tiled=True)
     spread = lax.all_to_all(grid_block, "gx", split_axis=2, concat_axis=1, tiled=True)
     local_first = jnp.einsum("sxyz,swyz->xw", spread, spread, precision=highest)
-    gram_first = lax.psum(local_first, ("gx", "gy", "gz"))
+    gram_first = jnp.sum(lax.all_gather(local_first, ("gx", "gy", "gz")), axis=0)
     factor_first = subspace(gram_first, start_first)
     rank_one = factor_first.shape[1]
     after_first = jnp.einsum("sxyz,xr->sryz", spread, factor_first, precision=highest)

time: 977 us -> 1590 us (1.63)
  waiting for transfers between devices: 790 us -> 1390 us
    all_gather x0 -> x1, waiting for transfers between devices: none -> 852 us  [shards(): lax.all_gather(local_first, ('gx', 'gy', 'gz'))]
    psum x1 -> x0, waiting for transfers between devices: 256 us -> none  [shards(): gram_first = lax.psum(local_first, ('gx', 'gy', 'gz'))]
where the time goes in v2:
time: 1590 us
  waiting for transfers between devices  1390 us (87%)
  blocking collectives  89.7 us (6%)
  other arithmetic  59 us (4%)
  matrix products  21.6 us (1%)
    all_gather x1, waiting for transfers between devices, shards(): lax.all_gather(local_first, ('gx', 'gy', 'gz'))  852 us
    psum x1, waiting for transfers between devices, shards(): gram_second = lax.psum(local_second, ('gx', 'gy', 'gz'))  270 us
    psum x1, waiting for transfers between devices, shards(): gram_third = lax.psum(local_third, ('gx', 'gy', 'gz'))  267 us
    all_to_all x1, blocking collectives, shards(): lax.all_to_all(grid_block, 'gx', split_axis=2, concat_axis=1, tiled=True)  39.6 us
  transfers between devices with their start and end apart: 3, of which 3 were waited for; matrix products, arithmetic and copies ran while one was open for 0% of the time, Pallas kernels for 0%

profile of v2, /device:TPU:24, one launch (start us, length us, event | category | flops | bytes accessed | tf_op | source)
XLA Modules:
  0.0 1587.3 jit_solution(10987002310511980648)
XLA Ops:
  10.6 20.2 %all_to_all.69 = f32[4,1,128,512]{2,0,1,3:T(4,128)S(1)} all-to-all(f32[4,1,128,512]{2,0,1,3:T(4,128)S(1)} %copy.38), channel_id=1, replica_groups=mesh['gx'=16,'gy'=4,'gz'=8] {'gz'}, dimensions={3} | all-to-all | bytes 2097152 | tf_op jit(solution)/shard_map/all_to_all | solution.py:39
  34.0 39.6 %all_to_all.70 = f32[16,1,16384]{2,1,0:T(1,128)S(1)} all-to-all(f32[16,1,16384]{2,1,0:T(1,128)S(1)} %reshape.63), channel_id=1, replica_groups=mesh['gx'=16,'gy'=4,'gz'=8] {'gx'}, dimensions={0} | all-to-all | bytes 2097152 | tf_op jit(solution)/shard_map/all_to_all | solution.py:40
  74.1 3.1 reduce.4
  78.1 2.6 copy.42
  82.9 2.4 convolution_bitcast_fusion.6
  85.4 852.2 %all-gather.3.cloned.1.call-done = f32[65536,128]{1,0:T(8,128)} async-done(((f32[128,128]{1,0:T(8,128)}), f32[65536,128]{1,0:T(8,128)}) %all-gather.3.cloned.1.call-update) | async-done | bytes 33554448 | tf_op jit(solution)/shard_map/all_gather | solution.py:42
  937.6 13.1 reduce_sum.9
  951.2 2.9 cholesky.104
  955.6 2.4 custom-call.12
  958.7 2.9 cholesky.115
  963.1 2.4 custom-call.13
  965.8 2.9 convolution_bitcast_fusion.3
  969.4 20.7 %all_to_all.71 = f32[64,1,1024]{2,1,0:T(1,128)S(1)} all-to-all(f32[64,1,1024]{2,1,0:T(1,128)S(1)} %reshape.65), channel_id=1, replica_groups=mesh['gx'=16,'gy'=4,'gz'=8] {'gx','gy'}, dimensions={0} | all-to-all | bytes 524288 | tf_op jit(solution)/shard_map/all_to_all | solution.py:47
  993.7 270.1 %all-reduce.3.cloned.1.call-done = f32[512,512]{1,0:T(8,128)} async-done(((f32[512,512]{1,0:T(8,128)}), f32[512,512]{1,0:T(8,128)}) %all-reduce.3.cloned.1.call-update) | async-done | bytes 1048592 | tf_op jit(solution)/shard_map/psum | solution.py:54
  1266.4 2.9 cholesky.126
  1270.8 2.4 custom-call.14
  1274.9 2.9 cholesky.137
  1279.3 2.4 custom-call.15
  1282.5 9.2 all_to_all.72
  1294.7 267.3 %all-reduce.5.cloned.1.call-done = f32[512,512]{1,0:T(8,128)} async-done(((f32[512,512]{1,0:T(8,128)}), f32[512,512]{1,0:T(8,128)}) %all-reduce.5.cloned.1.call-update) | async-done | bytes 1048592 | tf_op jit(solution)/shard_map/psum | solution.py:59
  1564.6 2.9 cholesky.148
  1568.9 2.4 custom-call.16
  1573.0 2.9 cholesky.159
  1577.3 2.4 custom-call.17
  (93 shorter events, 38.1 us)
Async XLA Ops:
  6.5 1257.2 %copy-start = (f32[512,32]{0,1:T(8,128)S(1)}, f32[512,32]{0,1:T(8,128)}, u32[]{:S(2)}) copy-start(f32[512,32]{0,1:T(8,128)} %param.13) | copy-start | bytes 196612
  6.5 1.6 copy-start.5
  6.5 931.1 %all-gather.3.cloned.1.call-start = ((), (), s32[]{:S(2)}) async-start(), calls=%async_computation.6 | async-start | bytes 33619968 | tf_op jit(solution)/shard_map/all_gather | solution.py:42
  85.3 1178.4 %all-reduce.3.cloned.1.call-start = ((), (), s32[]{:S(2)}) async-start(), calls=%async_computation.4 | async-start | bytes 2097152 | tf_op jit(solution)/shard_map/psum | solution.py:54
  937.6 13.1 copy-start.4
  993.6 568.4 %all-reduce.5.cloned.1.call-start = ((), (), s32[]{:S(2)}) async-start(), calls=%async_computation.5 | async-start | bytes 2097152 | tf_op jit(solution)/shard_map/psum | solution.py:59
  1263.7 9.8 copy-start.1
  1273.5 288.5 %copy-start.3 = (f32[512,32]{0,1:T(8,128)S(1)}, f32[512,32]{0,1:T(8,128)}, u32[]{:S(2)}) copy-start(f32[512,32]{0,1:T(8,128)} %param.14) | copy-start | bytes 196612
  1562.0 9.6 copy-start.2
Sparse Core Ops, SparseCore 0:
  85.5 852.1 all-gather.2
  993.7 269.9 all-reduce.2
  1294.8 267.1 all-reduce.4
